TPU v7x, 512 devices: a whole 4x8x8 slice. The times are simulated.
512 devices in a mesh: seq: 128 (over y, z, core), head: 4 (over x).
Axes of the slice: x: 4, y: 8, z: 8, core: 2. Of those that a mesh axis runs over, the one named last changes fastest.
Arguments:
- queries: bfloat16 [65536, 2048], P('seq', 'head'), may hold values from -4 to 4
- keys: bfloat16 [65536, 2048], P('seq', 'head'), may hold values from -4 to 4
- values: bfloat16 [65536, 2048], P('seq', 'head'), may hold values from -6 to 6
- rates: float32 [65536, 4], P('seq', 'head'), may hold values from 0.02 to 0.3
- fast: bfloat16 [4, 3, 512, 512], P('head'), may hold values from -0.25 to 0.25
- momentum: float32 [4, 3, 512, 512], P('head', None, 'seq'), may hold values from -0.24 to 0.24
- out_proj: bfloat16 [2048, 2048], P('seq', 'head'), may hold values from -0.125 to 0.125
Outputs:
- mixed: bfloat16 [65536, 2048], P('seq', 'head')
- new_momentum: float32 [4, 3, 512, 512], P('head', None, 'seq')
All inputs are finite; a program needn't handle non-finite values.
Results may differ from a plain program's by a relative error of at most 0.0094.
Values may be sent and summed in bfloat16 or wider, within the bound.
A program may use at most 64 MiB of HBM per device.

v0:
```python
import math
import jax
import jax.numpy as jnp
from jax import lax
from jax.sharding import PartitionSpec as P

HD = 512
WINDOW = 512
MOMENTUM_DECAY = 0.9
NORM_EPS = 1e-06
NEG_LARGE = -1e30


def from_behind(array, axis, by):
    devices = lax.axis_size(axis)
    pairs = [(i, i + by) for i in range(devices) if 0 <= i + by < devices]
    return lax.ppermute(array, axis, pairs)


def times_transposed(left, right):
    return lax.dot_general(
        left, right, (((1,), (1,)), ((), ())), preferred_element_type=jnp.float32
    )


def contract_rows(left, right):
    return lax.dot_general(
        left, right, (((0,), (0,)), ((), ())), preferred_element_type=jnp.float32
    )


def renormalize(base, moment):
    updated = base - moment
    base_rms = jnp.sqrt(jnp.mean(base * base, axis=-1, keepdims=True) + NORM_EPS)
    new_rms = jnp.sqrt(jnp.mean(updated * updated, axis=-1, keepdims=True) + NORM_EPS)
    return (updated * (base_rms / new_rms)).astype(jnp.bfloat16)


def shards(queries, keys, values, rates, fast, momentum, out_proj):
    tok_rows = queries.shape[0]
    ranks = lax.axis_size("seq")
    position = lax.axis_index("seq")
    own_rows = momentum.shape[2]
    grad_scale = 1.0 / math.sqrt(tok_rows * ranks)
    weights = fast[0]
    h_gate = times_transposed(keys, weights[0])
    h_up = times_transposed(keys, weights[1])
    sigma = jax.nn.sigmoid(h_gate)
    gated = (h_gate * sigma * h_up).astype(jnp.bfloat16)
    errors = (-grad_scale * rates * values.astype(jnp.float32)).astype(jnp.bfloat16)
    grad_down = contract_rows(errors, gated)
    back = jnp.dot(errors, weights[2], preferred_element_type=jnp.float32)
    d_gate = (back * h_up * sigma * (1.0 + h_gate * (1.0 - sigma))).astype(jnp.bfloat16)
    d_up = (back * h_gate * sigma).astype(jnp.bfloat16)
    grad_gate = contract_rows(d_gate, keys)
    grad_up = contract_rows(d_up, keys)
    grads = jnp.stack([grad_gate, grad_up, grad_down])
    row_start = position * own_rows
    placed = lax.dynamic_update_slice_in_dim(
        jnp.zeros(grads.shape, jnp.float32), MOMENTUM_DECAY * momentum[0], row_start, 1
    )
    moment_full = lax.psum(grads + placed, "seq")
    renewed = renormalize(weights.astype(jnp.float32), moment_full)
    moment_own = lax.dynamic_slice_in_dim(moment_full, row_start, own_rows, 1)
    q_gate = times_transposed(queries, renewed[0])
    q_up = times_transposed(queries, renewed[1])
    fast_in = (q_gate * jax.nn.sigmoid(q_gate) * q_up).astype(jnp.bfloat16)
    fast_out = times_transposed(fast_in, renewed[2])
    reach = (WINDOW + tok_rows - 2) // tok_rows
    stacked = jnp.stack([keys, values])
    earlier = [from_behind(stacked, "seq", 1)]
    extended = jnp.concatenate(earlier + [stacked], axis=1)
    key_count = extended.shape[1]
    key_pos = (position - reach) * tok_rows + jnp.arange(key_count)
    block = min(512, tok_rows)
    query_pos = position * tok_rows + 0 + jnp.arange(block)
    spacing = query_pos[:, None] - key_pos[None, :]
    allowed = (spacing >= 0) & (spacing < WINDOW) & (key_pos[None, :] >= 0)
    scores = times_transposed(queries, extended[0]) * (1.0 / math.sqrt(HD))
    scores = jnp.where(allowed, scores, NEG_LARGE)
    highest = jnp.max(scores, axis=1, keepdims=True)
    expo = jnp.exp(scores - highest)
    probs = (expo / jnp.sum(expo, axis=1, keepdims=True)).astype(jnp.bfloat16)
    attended_parts = jnp.dot(probs, extended[1], preferred_element_type=jnp.float32)
    combined = (attended_parts + fast_out).astype(jnp.bfloat16)
    all_heads = lax.all_gather(combined, "head", axis=1, tiled=True)
    projected = jnp.dot(
        all_heads,
        lax.all_gather(out_proj, "seq", axis=0, tiled=True),
        preferred_element_type=jnp.float32,
    )
    return (projected.astype(jnp.bfloat16), moment_own[None])


def solution(mesh):
    return jax.shard_map(
        shards,
        mesh=mesh,
        in_specs=(
            P("seq", "head"),
            P("seq", "head"),
            P("seq", "head"),
            P("seq", "head"),
            P("head", None, None, None),
            P("head", None, "seq", None),
            P("seq", "head"),
        ),
        out_specs=(P("seq", "head"), P("head", None, "seq", None)),
        check_vma=False,
    )
```

profile of v0, /device:TPU:1, one launch (start us, length us, event | category | flops | bytes accessed | tf_op | source)
XLA Modules:
  0.0 359.7 jit_solution(3982330911854318718)
XLA Ops:
  7.3 1.8 fusion.14
  9.6 0.5 fusion.18
  10.1 1.6 convolution_bitcast_fusion.2
  11.7 1.8 convolution_bitcast_fusion.4
  13.5 1.5 convolution_bitcast_fusion.3
  15.0 3.9 %pad_maximum_fusion = f32[3,512,512]{2,1,0:T(8,128)} fusion(f32[1,512,512]{2,1,0:T(8,128)} %convolution_bitcast_fusion.2, f32[1,512,512]{2,1,0:T(8,128)} %convolution_bitcast_fusion.3, f32[1,512,512]{2,1,0:T(8,128)} %convolution_bitcast_fusion.4), kind=kLoop, calls=%fused_computation.3 | loop fusion | flops 1572864 | bytes 6291456 | tf_op jit(solution)/shard_map/stack | solution.py:57
  18.9 1.4 fusion.26
  20.4 0.7 all-gather.5.cloned.1.call-update
  21.1 1.2 pad_maximum_fusion.1
  22.3 5.4 %collective-permute-start = (bf16[2,512,512]{2,1,0:T(8,128)(2,1)}, bf16[2,512,512]{2,1,0:T(8,128)(2,1)}, u32[]{:S(2)}, u32[]{:S(2)}) collective-permute-start(bf16[2,512,512]{2,1,0:T(8,128)(2,1)} %pad_maximum_fusion.1), channel_id=1, source_target_pairs={{0,4},{4,8},{8,12},{12,16},{16,20},{20,24},{24,28},{28,32},{32,36}... | collective-permute-start | bytes 3145736 | tf_op jit(solution)/shard_map/ppermute | solution.py:17
  27.7 12.2 %collective-permute-done = bf16[2,512,512]{2,1,0:T(8,128)(2,1)} collective-permute-done((bf16[2,512,512]{2,1,0:T(8,128)(2,1)}, bf16[2,512,512]{2,1,0:T(8,128)(2,1)}, u32[]{:S(2)}, u32[]{:S(2)}) %collective-permute-start) | collective-permute-done | bytes 1048608 | tf_op jit(solution)/shard_map/ppermute | solution.py:17
  39.9 1.4 maximum_maximum_fusion
  41.3 1.1 fusion.31
  42.7 1.3 copy-done.8
  44.4 185.0 %all-reduce.2.cloned.1.call-done = f32[3,512,512]{2,1,0:T(8,128)} async-done(((f32[3,512,512]{2,1,0:T(8,128)}), f32[3,512,512]{2,1,0:T(8,128)}) %all-reduce.2.cloned.1.call-update) | async-done | bytes 3145744 | tf_op jit(solution)/shard_map/psum | solution.py:62
  229.4 2.7 fusion
  232.7 1.2 copy-done.5
  233.8 1.5 convolution_bitcast_fusion.1
  235.3 3.5 fusion.7
  238.8 3.4 fusion.5
  242.2 1.4 dynamic-slice_bitcast_fusion
  243.7 70.2 %all-gather.5.cloned.1.call-done = bf16[2048,512]{1,0:T(8,128)(2,1)} async-done(((bf16[16,512]{1,0:T(8,128)(2,1)}), bf16[2048,512]{1,0:T(8,128)(2,1)}) %all-gather.5.cloned.1.call-update) | async-done | bytes 2097168 | tf_op jit(solution)/shard_map/all_gather | solution.py:89
  313.8 35.1 %all-gather.3.cloned.1.call-done = bf16[512,2048]{1,0:T(8,128)(2,1)} async-done(((bf16[512,512]{1,0:T(8,128)(2,1)}), bf16[512,2048]{1,0:T(8,128)(2,1)}) %all-gather.3.cloned.1.call-update) | async-done | bytes 2097168 | tf_op jit(solution)/shard_map/all_gather | solution.py:86
  348.9 4.3 %convolution_convert_fusion = bf16[512,512]{1,0:T(8,128)(2,1)} fusion(bf16[512,2048]{1,0:T(8,128)(2,1)} %all-gather.3.cloned.1.call-done, bf16[2048,512]{1,0:T(8,128)(2,1)} %all-gather.5.cloned.1.call-done), kind=kOutput, calls=%fused_computation.23 | convolution fusion | flops 1074003968 | bytes 4718592 | tf_op jit(solution)/shard_map/dot_general | solution.py:87
  (33 shorter events, 1.8 us)
Async XLA Ops:
  7.2 34.1 %copy-start = (bf16[512,512]{1,0:T(8,128)(2,1)S(1)}, bf16[512,512]{1,0:T(8,128)(2,1)}, u32[]{:S(2)}) copy-start(bf16[512,512]{1,0:T(8,128)(2,1)} %param.7) | copy-start | bytes 1572868
  7.2 1.9 copy-start.1
  7.2 1.9 copy-start.3
  7.2 222.2 %all-reduce.2.cloned.1.call-start = ((), (), s32[]{:S(2)}) async-start(), calls=%async_computation | async-start | bytes 6291456 | tf_op jit(solution)/shard_map/psum | solution.py:62
  7.2 2.3 copy-start.10
  7.3 2.3 copy-start.4
  15.0 3.9 %copy-start.9 = (f32[1,3,4,512]{3,2,1,0:T(4,128)S(1)}, f32[1,3,4,512]{3,2,1,0:T(4,128)}, u32[]{:S(2)}) copy-start(f32[1,3,4,512]{3,2,1,0:T(4,128)} %param.12) | copy-start | bytes 73732
  20.3 293.5 %all-gather.5.cloned.1.call-start = ((), (), s32[]{:S(2)}) async-start(), calls=%async_computation.2 | async-start | bytes 2113536 | tf_op jit(solution)/shard_map/all_gather | solution.py:89
  21.1 327.8 %all-gather.3.cloned.1.call-start = ((), (), s32[]{:S(2)}) async-start(), calls=%async_computation.1 | async-start | bytes 2621440 | tf_op jit(solution)/shard_map/all_gather | solution.py:86
  22.3 17.6 %collective-permute-start = (bf16[2,512,512]{2,1,0:T(8,128)(2,1)}, bf16[2,512,512]{2,1,0:T(8,128)(2,1)}, u32[]{:S(2)}, u32[]{:S(2)}) collective-permute-start(bf16[2,512,512]{2,1,0:T(8,128)(2,1)} %pad_maximum_fusion.1), channel_id=1, source_target_pairs={{0,4},{4,8},{8,12},{12,16},{16,20},{20,24},{24,28},{28,32},{32,36}... | collective-permute-start | bytes 3145736 | tf_op jit(solution)/shard_map/ppermute | solution.py:17
  41.3 1.4 copy-start.6
  42.7 1.3 copy-start.8
  229.4 2.8 copy-start.2
  232.7 1.2 copy-start.5
  235.3 3.5 copy-start.7
Sparse Core Ops, SparseCore 0:
  20.5 208.9 all-reduce.1
  232.5 81.2 all-gather.4
  316.5 32.3 all-gather.2
where the time goes:
time: 360 us
  waiting for transfers between devices  303 us (84%)
  matrix products  21.5 us (6%)
  between operations  13.9 us (4%)
  other arithmetic  11.3 us (3%)
  starting transfers between devices  5.49 us (2%)
  local copies, waits for them, and re-layouts  4.24 us (1%)
    psum x1, waiting for transfers between devices, shards(): moment_full = lax.psum(grads + placed, 'seq')  185 us
    all_gather x1, waiting for transfers between devices, shards(): lax.all_gather(out_proj, 'seq', axis=0, tiled=True)  70.2 us
    all_gather x1, waiting for transfers between devices, shards(): all_heads = lax.all_gather(combined, 'head', axis=1, tiled=True)  35.1 us
    ppermute x1, waiting for transfers between devices, from_behind(): return lax.ppermute(array, axis, pairs)  12.2 us
    dot_general x5, matrix products, times_transposed(): lax.dot_general(left, right, (((1,), (1,)), ((), ())), preferred_element_...  8.38 us
  transfers between devices with their start and end apart: 4, of which 4 were waited for; matrix products, arithmetic and copies ran while one was open for 5% of the time, Pallas kernels for 0%

commit v1 on v0

--- a/solution.py
+++ b/solution.py
@@ -86,7 +86,9 @@
     all_heads = lax.all_gather(combined, "head", axis=1, tiled=True)
     projected = jnp.dot(
         all_heads,
-        lax.all_gather(out_proj, "seq", axis=0, tiled=True),
+        jnp.concatenate(
+            lax.all_to_all(jnp.stack([out_proj] * lax.axis_size("seq")), "seq", 0, 0), axis=0
+        ),
         preferred_element_type=jnp.float32,
     )
     return (projected.astype(jnp.bfloat16), moment_own[None])

time: 360 us -> 328 us (0.911)
  waiting for transfers between devices: 303 us -> 253 us
  starting transfers between devices: 5.49 us -> 22 us
    all_gather x1 -> x0, waiting for transfers between devices: 70.2 us -> none  [shards(): lax.all_gather(out_proj, 'seq', axis=0, tiled=True)]
    psum x1, waiting for transfers between devices: 185 us -> 220 us  [shards(): moment_full = lax.psum(grads + placed, 'seq')]
    all_to_all x0 -> x1, starting transfers between devices: none -> 16.6 us  [shards(): lax.all_to_all(jnp.stack([out_proj] * lax.axis_size('seq')), 'seq', 0, 0)]
    ppermute x1, waiting for transfers between devices: 12.2 us -> 0.01 us  [from_behind(): return lax.ppermute(array, axis, pairs)]
  transfers between devices with their start and end apart: 4 -> 4, of which waited for: 4 -> 2; matrix products, arithmetic and copies ran while one was open for 5% -> 9% of each run, Pallas kernels for 0% -> 0%
where the time goes in v1:
time: 328 us
  waiting for transfers between devices  253 us (77%)
  starting transfers between devices  22 us (7%)
  matrix products  20.1 us (6%)
  between operations  14.2 us (4%)
  other arithmetic  12.6 us (4%)
  local copies, waits for them, and re-layouts  5.9 us (2%)
    psum x1, waiting for transfers between devices, shards(): moment_full = lax.psum(grads + placed, 'seq')  220 us
    all_gather x1, waiting for transfers between devices, shards(): all_heads = lax.all_gather(combined, 'head', axis=1, tiled=True)  32.4 us
    all_to_all x1, starting transfers between devices, shards(): lax.all_to_all(jnp.stack([out_proj] * lax.axis_size('seq')), 'seq', 0, 0)  16.6 us
    dot_general x5, matrix products, times_transposed(): lax.dot_general(left, right, (((1,), (1,)), ((), ())), preferred_element_...  6.99 us
  transfers between devices with their start and end apart: 4, of which 2 were waited for; matrix products, arithmetic and copies ran while one was open for 9% of the time, Pallas kernels for 0%

profile of v1, /device:TPU:1, one launch (start us, length us, event | category | flops | bytes accessed | tf_op | source)
XLA Modules:
  0.0 327.5 jit_solution(8029557780764490174)
XLA Ops:
  7.2 2.4 pad_maximum_fusion.1
  9.7 5.4 %collective-permute-start = (bf16[2,512,512]{2,1,0:T(8,128)(2,1)}, bf16[2,512,512]{2,1,0:T(8,128)(2,1)}, u32[]{:S(2)}, u32[]{:S(2)}) collective-permute-start(bf16[2,512,512]{2,1,0:T(8,128)(2,1)} %pad_maximum_fusion.1), channel_id=1, source_target_pairs={{0,4},{4,8},{8,12},{12,16},{16,20},{20,24},{24,28},{28,32},{32,36}... | collective-permute-start | bytes 3145736 | tf_op jit(solution)/shard_map/ppermute | solution.py:17
  15.1 0.5 fusion.14
  15.6 0.5 fusion.16
  16.1 0.5 fusion.18
  16.6 1.6 convolution_bitcast_fusion.2
  18.3 1.8 convolution_bitcast_fusion.4
  20.0 1.5 convolution_bitcast_fusion.3
  21.6 3.9 %pad_maximum_fusion = f32[3,512,512]{2,1,0:T(8,128)} fusion(f32[1,512,512]{2,1,0:T(8,128)} %convolution_bitcast_fusion.2, f32[1,512,512]{2,1,0:T(8,128)} %convolution_bitcast_fusion.3, f32[1,512,512]{2,1,0:T(8,128)} %convolution_bitcast_fusion.4), kind=kLoop, calls=%fused_computation.3 | loop fusion | flops 1572864 | bytes 6291456 | tf_op jit(solution)/shard_map/stack | solution.py:57
  25.4 1.4 fusion.26
  26.9 1.6 stack.26
  28.5 16.6 %all-to-all-start = ((bf16[128,16,512]{2,1,0:T(8,128)(2,1)}), bf16[128,16,512]{2,1,0:T(8,128)(2,1)}, u32[]{:S(2)}, u32[]{:S(2)}) async-start(bf16[128,16,512]{2,1,0:T(8,128)(2,1)} %stack.26), calls=%async_computation | async-start | bytes 4194304 | tf_op jit(solution)/shard_map/all_to_all | solution.py:90
  45.2 1.4 maximum_maximum_fusion
  46.6 1.1 fusion.31
  47.9 1.3 copy-done.8
  49.6 220.2 %all-reduce.2.cloned.1.call-done = f32[3,512,512]{2,1,0:T(8,128)} async-done(((f32[3,512,512]{2,1,0:T(8,128)}), f32[3,512,512]{2,1,0:T(8,128)}) %all-reduce.2.cloned.1.call-update) | async-done | bytes 3145744 | tf_op jit(solution)/shard_map/psum | solution.py:62
  269.8 2.7 fusion
  273.1 1.2 copy-done.5
  274.2 1.5 convolution_bitcast_fusion.1
  275.7 3.5 %fusion.7 = f32[512,512]{1,0:T(8,128)} fusion(bf16[512,512]{1,0:T(8,128)(2,1)S(1)} %copy-done, f32[512,512]{1,0:T(8,128)} %convolution_bitcast_fusion.1, bf16[3,512,512]{2,1,0:T(8,128)(2,1)} %copy-done.5), kind=kOutput, calls=%fused_computation.25 | convolution fusion | flops 538443776 | bytes 3670016 | tf_op jit(solution)/shard_map/dot_general | solution.py:21
  279.2 3.4 %fusion.5 = bf16[512,512]{1,0:T(8,128)(2,1)} fusion(f32[512,512]{1,0:T(8,128)} %fusion.7, bf16[2,1024,512]{2,1,0:T(8,128)(2,1)S(1)} %copy-done.7, f32[512,1024]{0,1:T(8,128)} %copy-done.8, f32[512]{0:T(512)S(1)} %fusion.3, f32[512]{0:T(512)S(1)} %get-tuple-element.4), kind=kOutput, calls=%fused_computation.22 | convolution fusion | flops 538968064 | bytes 4722688 | tf_op jit(solution)/shard_map/dot_general | solution.py:84
  282.6 1.4 dynamic-slice_bitcast_fusion
  284.0 32.4 %all-gather.2.cloned.1.call-done = bf16[512,2048]{1,0:T(8,128)(2,1)} async-done(((bf16[512,512]{1,0:T(8,128)(2,1)}), bf16[512,2048]{1,0:T(8,128)(2,1)}) %all-gather.2.cloned.1.call-update) | async-done | bytes 2097168 | tf_op jit(solution)/shard_map/all_gather | solution.py:86
  316.4 4.3 %convolution_convert_fusion = bf16[512,512]{1,0:T(8,128)(2,1)} fusion(bf16[512,2048]{1,0:T(8,128)(2,1)} %all-gather.2.cloned.1.call-done, bf16[2048,512]{1,0:T(8,128)(2,1)} %bitcast.20), kind=kOutput, calls=%fused_computation.23 | convolution fusion | flops 1074003968 | bytes 4718592 | tf_op jit(solution)/shard_map/dot_general | solution.py:87
  (35 shorter events, 1.3 us)
Async XLA Ops:
  7.2 39.4 %copy-start = (bf16[512,512]{1,0:T(8,128)(2,1)S(1)}, bf16[512,512]{1,0:T(8,128)(2,1)}, u32[]{:S(2)}) copy-start(bf16[512,512]{1,0:T(8,128)(2,1)} %param.7) | copy-start | bytes 1572868
  7.2 7.9 %copy-start.3 = (bf16[512,512]{1,0:T(8,128)(2,1)S(1)}, bf16[512,512]{1,0:T(8,128)(2,1)}, u32[]{:S(2)}) copy-start(bf16[512,512]{1,0:T(8,128)(2,1)} %param.8) | copy-start | bytes 1572868
  7.2 7.9 %copy-start.1 = (bf16[1,3,512,512]{3,2,1,0:T(8,128)(2,1)S(1)}, bf16[1,3,512,512]{3,2,1,0:T(8,128)(2,1)}, u32[]{:S(2)}) copy-start(bf16[1,3,512,512]{3,2,1,0:T(8,128)(2,1)} %param.11) | copy-start | bytes 4718596
  7.2 262.6 %all-reduce.2.cloned.1.call-start = ((), (), s32[]{:S(2)}) async-start(), calls=%async_computation.1 | async-start | bytes 6291456 | tf_op jit(solution)/shard_map/psum | solution.py:62
  9.7 35.5 %collective-permute-start = (bf16[2,512,512]{2,1,0:T(8,128)(2,1)}, bf16[2,512,512]{2,1,0:T(8,128)(2,1)}, u32[]{:S(2)}, u32[]{:S(2)}) collective-permute-start(bf16[2,512,512]{2,1,0:T(8,128)(2,1)} %pad_maximum_fusion.1), channel_id=1, source_target_pairs={{0,4},{4,8},{8,12},{12,16},{16,20},{20,24},{24,28},{28,32},{32,36}... | collective-permute-start | bytes 3145736 | tf_op jit(solution)/shard_map/ppermute | solution.py:17
  15.1 1.0 copy-start.11
  15.1 1.0 copy-start.4
  21.6 3.9 %copy-start.9 = (f32[1,3,4,512]{3,2,1,0:T(4,128)S(1)}, f32[1,3,4,512]{3,2,1,0:T(4,128)}, u32[]{:S(2)}) copy-start(f32[1,3,4,512]{3,2,1,0:T(4,128)} %param.12) | copy-start | bytes 73732
  25.4 1.5 copy-start.10
  28.5 255.5 %all-to-all-start = ((bf16[128,16,512]{2,1,0:T(8,128)(2,1)}), bf16[128,16,512]{2,1,0:T(8,128)(2,1)}, u32[]{:S(2)}, u32[]{:S(2)}) async-start(bf16[128,16,512]{2,1,0:T(8,128)(2,1)} %stack.26), calls=%async_computation | async-start | bytes 4194304 | tf_op jit(solution)/shard_map/all_to_all | solution.py:90
  45.1 271.3 %all-gather.2.cloned.1.call-start = ((), (), s32[]{:S(2)}) async-start(), calls=%async_computation.2 | async-start | bytes 2621440 | tf_op jit(solution)/shard_map/all_gather | solution.py:86
  46.6 1.3 copy-start.6
  47.9 1.3 copy-start.8
  269.8 2.8 copy-start.2
  273.1 1.2 copy-start.5
  275.7 3.5 %copy-start.7 = (bf16[2,1024,512]{2,1,0:T(8,128)(2,1)S(1)}, bf16[2,1024,512]{2,1,0:T(8,128)(2,1)}, u32[]{:S(2)}) copy-start(bf16[2,1024,512]{2,1,0:T(8,128)(2,1)} %copy-done.6) | copy-start | bytes 6291460
Sparse Core Ops, SparseCore 0:
  27.0 242.7 all-reduce.1
  282.7 33.6 all-gather.1
